TPU v7x, 256 devices: a whole 4x4x8 slice. The times are simulated.
256 devices in a mesh: row: 32 (over y, z), col: 8 (over x, core).
Axes of the slice: x: 4, y: 4, z: 8, core: 2. Of those that a mesh axis runs over, the one named last changes fastest.
Arguments:
- responses: bfloat16 [4096, 2, 3, 2048], P(('col', 'row')), may hold values from -6 to 6
- labels: int32 [2048], replicated, may hold values from 0 to 15
- conductivity: float32 [16], replicated, may hold values from 0.05 to 2
- permittivity: float32 [16], replicated, may hold values from 0.1 to 1.6
Outputs:
- noise_cov: float32 [2, 4096, 4096], P(None, 'row', 'col')
- energy_gram: float32 [2, 4096, 4096], P(None, 'row', 'col')
All inputs are finite; a program needn't handle non-finite values.
Results may differ from a plain program's by a relative error of at most 0.0021.
Values may be sent and summed in bfloat16 or wider, within the bound.
No kernel may reach another device: no remote copies, remote signals or barrier semaphores. Data moves between devices by JAX's collectives and lax.ppermute only.
A program may use at most 128 MiB of HBM per device.

v0:
```python
import jax
import jax.numpy as jnp
from jax import lax
from jax.sharding import PartitionSpec as P


def broadcast(block, axis, holder):
    block = jnp.where(lax.axis_index(axis) == holder, block, jnp.zeros_like(block))
    return lax.psum(block, axis)


def tile_products(row_fields, right_fields, vox_labels, conductivity, permittivity, scale_factor):
    classes = jnp.arange(conductivity.shape[0], dtype=jnp.int32)
    onehot = (vox_labels[None, :] == classes[:, None]).astype(jnp.float32)
    cond_voxel = jnp.sum(onehot * conductivity[:, None], axis=0) * scale_factor
    perm_voxel = jnp.sum(onehot * permittivity[:, None], axis=0) * scale_factor
    fields = row_fields.astype(jnp.float32)
    vox_here = row_fields.shape[3]
    row_total = row_fields.shape[0]

    def weighted(weight_vec):
        scaled = fields * weight_vec[None, None, None, :]
        crossed = jnp.concatenate([-scaled[:, 1:2], scaled[:, 0:1]], axis=1)
        return (scaled.astype(jnp.bfloat16), crossed.astype(jnp.bfloat16))

    sig_plain, sig_cross = weighted(cond_voxel)
    eps_plain, eps_cross = weighted(perm_voxel)
    left_stack = jnp.concatenate([sig_plain, sig_cross, eps_plain, eps_cross], axis=0)
    left_stack = left_stack.reshape(4 * row_total, 6 * vox_here)
    right_flat = right_fields.reshape(right_fields.shape[0], 6 * vox_here)
    products = lax.dot_general(
        left_stack, right_flat, (((1,), (1,)), ((), ())), preferred_element_type=jnp.float32
    )
    return products.reshape(4, row_total, right_fields.shape[0])


def body(responses, labels, conductivity, permittivity):
    nb_dev = responses.shape[0]
    vox_total = labels.shape[0]
    row_count = lax.axis_size("row")
    col_count = lax.axis_size("col")
    row_block = nb_dev * col_count
    row_index = lax.axis_index("row")
    scale_factor = 1.0 / jnp.sqrt(jnp.float32(6 * vox_total))
    columns = lax.all_gather(responses, "row", axis=0, tiled=True)
    row_ratio = row_count // col_count
    own_rows = lax.dynamic_slice_in_dim(columns, row_index % row_ratio * row_block, row_block, 0)
    row_fields = broadcast(own_rows, "col", row_index // row_ratio)
    products = tile_products(row_fields, columns, labels, conductivity, permittivity, scale_factor)
    noise_cov = products[0:2]
    energy_gram = products[2:4]
    return (noise_cov, energy_gram)


def solution(mesh):
    in_specs = (P(("col", "row"), None, None, None), P(), P(), P())
    out_specs = (P(None, "row", "col"), P(None, "row", "col"))
    return jax.shard_map(body, mesh=mesh, in_specs=in_specs, out_specs=out_specs, check_vma=False)
```

profile of v0, /device:TPU:8, one launch (start us, length us, event | category | flops | bytes accessed | tf_op | source)
XLA Modules:
  0.0 240.6 jit_solution(9226071765441624125)
XLA Ops:
  7.2 0.0 copy-start.4
  7.2 0.0 copy-start.3
  7.2 0.0 copy-start.2
  7.2 0.0 all-gather.2.cloned.1.call-start
  7.2 1.9 copy.7
  9.1 0.0 all-gather.2.cloned.1.call-update
  9.1 0.0 all-reduce.2.cloned.1.call-start
  9.2 123.3 %all-gather.2.cloned.1.call-done = bf16[512,2,3,2048]{3,0,2,1:T(8,128)(2,1)} async-done(((bf16[16,2,3,2048]{3,0,2,1:T(8,128)(2,1)}), bf16[512,2,3,2048]{3,0,2,1:T(8,128)(2,1)}) %all-gather.2.cloned.1.call-update) | async-done | bytes 12582928 | tf_op jit(solution)/shard_map/all_gather | solution.py:45
  132.5 4.5 %dynamic-slice_select_fusion = bf16[128,2,3,2048]{3,0,2,1:T(8,128)(2,1)} fusion(bf16[512,2,3,2048]{3,0,2,1:T(8,128)(2,1)} %all-gather.2.cloned.1.call-done, s32[]{:T(128)S(6)} %select_n.25, pred[]{:T(512)S(6)} %eq.18), kind=kLoop, calls=%fused_computation.18 | loop fusion | flops 1572864 | bytes 6291461 | tf_op jit(solution)/shard_map/jit(_where)/select_n | solution.py:8
  137.0 0.0 all-reduce.2.cloned.1.call-update
  137.0 0.0 copy-done.4
  137.0 0.0 copy-done.3
  137.1 0.0 copy-done.2
  137.1 0.1 select_reduce_fusion.1
  137.2 72.5 %all-reduce.2.cloned.1.call-done = bf16[128,2,3,2048]{3,0,2,1:T(8,128)(2,1)} async-done(((bf16[128,2,3,2048]{3,0,2,1:T(8,128)(2,1)}), bf16[128,2,3,2048]{3,0,2,1:T(8,128)(2,1)}) %all-reduce.2.cloned.1.call-update) | async-done | bytes 3145744 | tf_op jit(solution)/shard_map/psum | solution.py:9
  209.7 6.8 %convert_multiply_fusion.1 = (f32[128,2,3,2048]{3,0,2,1:T(8,128)S(1)}, bf16[128,2,3,2048]{3,0,2,1:T(8,128)(2,1)}, bf16[128,2,3,2048]{3,0,2,1:T(8,128)(2,1)}, f32[128,2,3,2048]{3,0,2,1:T(8,128)S(1)}) fusion(bf16[128,2,3,2048]{3,0,2,1:T(8,128)(2,1)} %all-reduce.2.cloned.1.call-done, f32[2048]{0:T(1024)S(1)} %get-tuple-element.13, f32[2048]{0:T(1024)S(1)} %get-tuple-element.12), kind=kLoop, calls=%fused_computation.13 | loop fusion | flops 7864320 | bytes 22036480 | tf_op jit(solution)/shard_map/mul | solution.py:22
  216.5 0.0 copy-start
  216.5 0.0 copy-start.1
  216.5 0.2 fusion.13
  216.7 0.2 fusion.12
  217.0 1.4 copy-done
  218.4 0.2 slice.35
  218.5 0.8 copy-done.1
  219.3 0.2 slice.37
  219.5 13.2 %fusion.14 = f32[512,512]{1,0:T(8,128)S(1)} fusion(bf16[512,2,3,2048]{3,0,2,1:T(8,128)(2,1)} %all-gather.2.cloned.1.call-done, bf16[128,1,3,2048]{3,0,2,1:T(8,128)(2,1)S(1)} %slice.37, bf16[128,1,3,2048]{3,0,2,1:T(8,128)(2,1)S(1)} %fusion.12, bf16[128,2,3,2048]{3,0,2,1:T(8,128)(2,1)S(1)} %copy-done.1, bf16[128,1,3,2048]{3,0,2,1:T(8,128)(2,1)S(1)} %slice.35, ...), kind=kOutput, calls=%fused_computation.19 | convolution fusion | flops 6517948416 | bytes 26214400 | tf_op jit(solution)/shard_map/dot_general | solution.py:31
  232.7 1.0 fusion.20
  (1 shorter events, 0.0 us)
Async XLA Ops:
  7.2 129.9 %copy-start.4 = (f32[16]{0:T(128)S(1)}, f32[16]{0:T(128)}, u32[]{:S(2)}) copy-start(f32[16]{0:T(128)} %param.7) | copy-start | bytes 196
  7.2 129.9 %copy-start.3 = (f32[16]{0:T(128)S(1)}, f32[16]{0:T(128)}, u32[]{:S(2)}) copy-start(f32[16]{0:T(128)} %param.6) | copy-start | bytes 196
  7.2 129.9 %copy-start.2 = (s32[2048]{0:T(1024)S(1)}, s32[2048]{0:T(1024)}, u32[]{:S(2)}) copy-start(s32[2048]{0:T(1024)} %param.5) | copy-start | bytes 24580
  7.2 125.3 %all-gather.2.cloned.1.call-start = ((), (), s32[]{:S(2)}) async-start(), calls=%async_computation | async-start | bytes 12976128 | tf_op jit(solution)/shard_map/all_gather | solution.py:45
  9.1 200.5 %all-reduce.2.cloned.1.call-start = ((), (), s32[]{:S(2)}) async-start(), calls=%async_computation.1 | async-start | bytes 6291456 | tf_op jit(solution)/shard_map/psum | solution.py:9
  216.5 1.9 copy-start
  216.5 2.8 %copy-start.1 = (bf16[128,2,3,2048]{3,0,2,1:T(8,128)(2,1)S(1)}, bf16[128,2,3,2048]{3,0,2,1:T(8,128)(2,1)}, u32[]{:S(2)}) copy-start(bf16[128,2,3,2048]{3,0,2,1:T(8,128)(2,1)} %get-tuple-element.8) | copy-start | bytes 9437188
Sparse Core Ops, SparseCore 0:
  11.2 121.3 all-gather.1
  137.2 72.4 all-reduce.1
where the time goes:
time: 241 us
  waiting for transfers between devices  196 us (81%)
  between operations  14.2 us (6%)
  matrix products  13.2 us (5%)
  other arithmetic  11.9 us (5%)
  local copies, waits for them, and re-layouts  5.42 us (2%)
    all_gather x1, waiting for transfers between devices, body(): columns = lax.all_gather(responses, 'row', axis=0, tiled=True)  123 us
    psum x1, waiting for transfers between devices, broadcast(): return lax.psum(block, axis)  72.5 us
    dot_general x1, matrix products, tile_products(): lax.dot_general(left_stack, right_flat, (((1,), (1,)), ((), ())), preferr...  13.2 us
    mul x1, other arithmetic, weighted(): scaled = fields * weight_vec[None, None, None, :]  6.83 us
  transfers between devices with their start and end apart: 2, of which 2 were waited for; matrix products, arithmetic and copies ran while one was open for 0% of the time, Pallas kernels for 0%

commit v1 on v0

--- a/solution.py
+++ b/solution.py
@@ -42,7 +42,12 @@
     row_block = nb_dev * col_count
     row_index = lax.axis_index("row")
     scale_factor = 1.0 / jnp.sqrt(jnp.float32(6 * vox_total))
-    columns = lax.all_gather(responses, "row", axis=0, tiled=True)
+    columns = jnp.concatenate(
+        lax.all_to_all(
+            jnp.stack([responses] * lax.axis_size("row")), "row", split_axis=0, concat_axis=0
+        ),
+        axis=0,
+    )
     row_ratio = row_count // col_count
     own_rows = lax.dynamic_slice_in_dim(columns, row_index % row_ratio * row_block, row_block, 0)
     row_fields = broadcast(own_rows, "col", row_index // row_ratio)

time: 241 us -> 467 us (1.94)
  waiting for transfers between devices: 196 us -> 330 us
  local copies, waits for them, and re-layouts: 5.42 us -> 79.2 us
  starting transfers between devices: 0.08 us -> 11.8 us
  other arithmetic: 11.9 us -> 17.4 us
    all_to_all x0 -> x1, waiting for transfers between devices: none -> 295 us  [body(): lax.all_to_all(jnp.stack([responses] * lax.axis_size('row')), 'row', spli...]
    all_gather x1 -> x0, waiting for transfers between devices: 123 us -> none  [body(): columns = lax.all_gather(responses, 'row', axis=0, tiled=True)]
    psum x1, waiting for transfers between devices: 72.5 us -> 34.7 us  [broadcast(): return lax.psum(block, axis)]
    another operation x0 -> x2, local copies, waits for them, and re-layouts: none -> 35.7 us  [the longest x1 29.6 us: tile_products(): right_flat = right_fields.reshape(right_fields.shape[0], 6 * vox_here)]
    all_to_all x0 -> x2, local copies, waits for them, and re-layouts: none -> 24.3 us  [body(): lax.all_to_all(jnp.stack([responses] * lax.axis_size('row')), 'row', spli...]
    concatenate x0 -> x1, local copies, waits for them, and re-layouts: none -> 16.7 us  [tile_products(): jnp.concatenate([sig_plain, sig_cross, eps_plain, eps_cross], axis=0)]
    all_to_all x0 -> x1, starting transfers between devices: none -> 11.8 us  [body(): lax.all_to_all(jnp.stack([responses] * lax.axis_size('row')), 'row', spli...]
    concatenate x0 -> x1, other arithmetic: none -> 5.58 us  [tile_products(): jnp.concatenate([sig_plain, sig_cross, eps_plain, eps_cross], axis=0)]
  transfers between devices with their start and end apart: 2 -> 2, of which waited for: 2 -> 2; matrix products, arithmetic and copies ran while one was open for 0% -> 10% of each run, Pallas kernels for 0% -> 0%
where the time goes in v1:
time: 467 us; the launch traced here: 466 us
  waiting for transfers between devices  330 us (71%)
  local copies, waits for them, and re-layouts  79.2 us (17%)
  other arithmetic  17.4 us (4%)
  between operations  14.2 us (3%)
  matrix products  13.4 us (3%)
  starting transfers between devices  11.8 us (3%)
    all_to_all x1, waiting for transfers between devices, body(): lax.all_to_all(jnp.stack([responses] * lax.axis_size('row')), 'row', spli...  295 us
    psum x1, waiting for transfers between devices, broadcast(): return lax.psum(block, axis)  34.7 us
    another operation x1, local copies, waits for them, and re-layouts, tile_products(): right_flat = right_fields.reshape(right_fields.shape[0], 6 * vox_here)  29.6 us
    all_to_all x2, local copies, waits for them, and re-layouts, body(): lax.all_to_all(jnp.stack([responses] * lax.axis_size('row')), 'row', spli...  24.3 us
    concatenate x1, local copies, waits for them, and re-layouts, tile_products(): jnp.concatenate([sig_plain, sig_cross, eps_plain, eps_cross], axis=0)  16.7 us
    dot_general x1, matrix products, tile_products(): lax.dot_general(left_stack, right_flat, (((1,), (1,)), ((), ())), preferr...  13.4 us
    all_to_all x1, starting transfers between devices, body(): lax.all_to_all(jnp.stack([responses] * lax.axis_size('row')), 'row', spli...  11.8 us
  transfers between devices with their start and end apart: 2, of which 2 were waited for; matrix products, arithmetic and copies ran while one was open for 10% of the time, Pallas kernels for 0%

profile of v1, /device:TPU:8, one launch (start us, length us, event | category | flops | bytes accessed | tf_op | source)
XLA Modules:
  0.0 465.5 jit_solution(7724721392845449087)
XLA Ops:
  7.2 1.1 copy.16
  8.3 6.1 %stack.2 = bf16[32,16,2,3,2048]{4,1,3,2,0:T(8,128)(2,1)} broadcast(bf16[16,2,3,2048]{3,0,2,1:T(8,128)(2,1)S(1)} %copy.16), dimensions={1,2,3,4} | broadcast | bytes 12976128 | tf_op jit(solution)/shard_map/stack | solution.py:47
  14.4 11.8 %all-to-all-start = ((bf16[32,16,2,3,2048]{4,1,3,2,0:T(8,128)(2,1)}), bf16[32,16,2,3,2048]{4,1,3,2,0:T(8,128)(2,1)}, u32[]{:S(2)}, u32[]{:S(2)}) async-start(bf16[32,16,2,3,2048]{4,1,3,2,0:T(8,128)(2,1)} %stack.2), calls=%async_computation | async-start | bytes 25165824 | tf_op jit(solution)/shard_map/all_to_all | solution.py:46
  26.1 0.0 all-reduce.2.cloned.1.call-start
  26.2 294.8 %all-to-all-done = bf16[32,16,2,3,2048]{4,1,3,2,0:T(8,128)(2,1)} async-done(((bf16[32,16,2,3,2048]{4,1,3,2,0:T(8,128)(2,1)}), bf16[32,16,2,3,2048]{4,1,3,2,0:T(8,128)(2,1)}, u32[]{:S(2)}, u32[]{:S(2)}) %all-to-all-start) | async-done | bytes 12582944 | tf_op jit(solution)/shard_map/all_to_all | solution.py:46
  321.0 6.5 %copy.17 = bf16[32,16,2,3,2048]{4,1,0,3,2:T(8,128)(2,1)S(1)} copy(bf16[32,16,2,3,2048]{4,1,3,2,0:T(8,128)(2,1)} %all-to-all-done) | data formatting | bytes 25165824 | tf_op jit(solution)/shard_map/all_to_all | solution.py:46
  327.5 0.0 copy-start
  327.5 0.0 copy-start.1
  327.5 0.0 copy-start.2
  327.5 2.6 dynamic-slice_select_fusion
  330.1 0.0 all-reduce.2.cloned.1.call-update
  330.1 0.0 copy-done
  330.1 0.0 copy-done.1
  330.1 0.0 copy-done.2
  330.1 0.1 select_reduce_fusion.1
  330.3 17.8 %copy.19 = bf16[32,16,2,3,2048]{4,3,2,1,0:T(4,128)(2,1)} copy(bf16[32,16,2,3,2048]{4,1,3,2,0:T(8,128)(2,1)} %all-to-all-done) | data formatting | bytes 25165824 | tf_op jit(solution)/shard_map/all_to_all | solution.py:46
  348.0 29.6 %reshape_reshape.3 = bf16[512,12288]{1,0:T(8,128)(2,1)} reshape(bf16[32,16,2,3,2048]{4,3,2,1,0:T(4,128)(2,1)} %copy.19) | data formatting | bytes 25165824 | tf_op jit(solution)/shard_map/reshape;reshape | solution.py:30
  377.7 34.7 %all-reduce.2.cloned.1.call-done = bf16[128,2,3,2048]{3,0,2,1:T(8,128)(2,1)} async-done(((bf16[128,2,3,2048]{3,0,2,1:T(8,128)(2,1)}), bf16[128,2,3,2048]{3,0,2,1:T(8,128)(2,1)}) %all-reduce.2.cloned.1.call-update) | async-done | bytes 3145744 | tf_op jit(solution)/shard_map/psum | solution.py:9
  412.4 6.8 %convert_multiply_fusion.1 = (f32[128,2,3,2048]{3,0,2,1:T(8,128)}, bf16[128,2,3,2048]{3,0,2,1:T(8,128)(2,1)S(1)}, bf16[128,2,3,2048]{3,0,2,1:T(8,128)(2,1)S(1)}, f32[128,2,3,2048]{3,0,2,1:T(8,128)S(1)}) fusion(bf16[128,2,3,2048]{3,0,2,1:T(8,128)(2,1)} %all-reduce.2.cloned.1.call-done, f32[2048]{0:T(1024)S(1)} %get-tuple-element.13, f32[2048]{0:T(1024)S(1)} %get-tuple-element.12), kind=kLoop, calls=%fused_computation.2 | loop fusion | flops 7864320 | bytes 22036480 | tf_op jit(solution)/shard_map/mul | solution.py:22
  419.2 2.1 fusion.1
  421.3 0.2 fusion
  421.6 0.2 slice.35
  421.8 0.2 slice.37
  422.0 5.6 %maximum_maximum_fusion = bf16[512,2,3,2048]{3,0,2,1:T(8,128)(2,1)} fusion(bf16[128,1,3,2048]{3,0,2,1:T(8,128)(2,1)S(1)} %slice.37, bf16[128,1,3,2048]{3,0,2,1:T(8,128)(2,1)S(1)} %fusion, bf16[128,2,3,2048]{3,0,2,1:T(8,128)(2,1)S(1)} %get-tuple-element.8, bf16[128,1,3,2048]{3,0,2,1:T(8,128)(2,1)S(1)} %slice.35, bf16[128,1,3,2048]{3,0,2,1:T(8,128)(2,1)S(1)} %fusion.1, ...), kind=kLoop, calls=%fused_computation | loop fusion | flops 75497472 | bytes 25165824 | tf_op jit(solution)/shard_map/concatenate | solution.py:28
  427.5 16.7 %copy.18 = bf16[512,2,3,2048]{0,3,2,1:T(8,128)(2,1)} copy(bf16[512,2,3,2048]{3,0,2,1:T(8,128)(2,1)} %maximum_maximum_fusion) | data formatting | bytes 25165824 | tf_op jit(solution)/shard_map/concatenate | solution.py:28
  444.2 13.4 %fusion.5 = f32[512,512]{1,0:T(8,128)S(1)} fusion(bf16[512,12288]{0,1:T(8,128)(2,1)} %bitcast.7, bf16[512,12288]{1,0:T(8,128)(2,1)} %reshape_reshape.3), kind=kOutput, calls=%fused_computation.16 | convolution fusion | flops 6442450944 | bytes 26214400 | tf_op jit(solution)/shard_map/dot_general | solution.py:31
  457.6 1.0 fusion.4
  (1 shorter events, 0.0 us)
Async XLA Ops:
  14.4 306.6 %all-to-all-start = ((bf16[32,16,2,3,2048]{4,1,3,2,0:T(8,128)(2,1)}), bf16[32,16,2,3,2048]{4,1,3,2,0:T(8,128)(2,1)}, u32[]{:S(2)}, u32[]{:S(2)}) async-start(bf16[32,16,2,3,2048]{4,1,3,2,0:T(8,128)(2,1)} %stack.2), calls=%async_computation | async-start | bytes 25165824 | tf_op jit(solution)/shard_map/all_to_all | solution.py:46
  26.1 386.3 %all-reduce.2.cloned.1.call-start = ((), (), s32[]{:S(2)}) async-start(), calls=%async_computation.1 | async-start | bytes 6291456 | tf_op jit(solution)/shard_map/psum | solution.py:9
  327.5 2.6 copy-start
  327.5 2.6 copy-start.1
  327.5 2.6 copy-start.2
Sparse Core Ops, SparseCore 0:
  330.2 82.1 all-reduce.1
